TPU v7x, 32 devices: a whole 2x2x4 slice. The times are simulated.
32 devices in a mesh: gz: 4 (over z), gy: 2 (over x), vec: 4 (over y, core).
Axes of the slice: x: 2, y: 2, z: 4, core: 2. Of those that a mesh axis runs over, the one named last changes fastest.
Arguments:
- vectors: bfloat16 [256, 3, 32, 4, 128], P('vec', None, 'gz', 'gy'), may hold values from -6 to 6
- links: bfloat16 [3, 3, 3, 32, 4, 128], P(None, None, None, 'gz', 'gy'), may hold values from -4 to 4
- momentum: int32 [3], replicated, may hold values from -5 to 5, as said below
- directions: int32 [3], replicated, may hold values from 0 to 2, each once
Outputs:
- elementals: float32 [4, 2, 256, 256], P(None, None, 'vec')
Inputs may be any that keep to these rules, and one draw needn't show every extreme that they name: `momentum`: one component is -5, another 5. `directions`: each of 0, 1, 2 once.
All inputs are finite; a program needn't handle non-finite values.
Results may differ from a plain program's by a relative error of at most 0.0029.
Values may be sent and summed in bfloat16 or wider, within the bound.
A program may use at most 128 MiB of HBM per device.

v0:
```python
import functools
import math

import jax
import jax.numpy as jnp
from jax import lax
from jax.experimental import pallas as pl
from jax.experimental.pallas import tpu as pltpu
from jax.sharding import PartitionSpec as P

MESH = pl.DeviceIdType.MESH


def split_chunks(depth, most):
    count = most
    while depth % count:
        count -= 1
    return count


def kernel(
    sizes,
    momentum_in,
    directions_in,
    v_ref,
    links_ref,
    links_far,
    out_ref,
    ext,
    left,
    rim_y,
    rim_z,
    tab_x,
    tab_y,
    tab_z,
    cos_ref,
    sin_ref,
    trans,
    acc,
    momentum_ref,
    directions_ref,
    outgo,
    income,
    reduced,
    gathered,
    local_sem,
    send_sem,
    recv_sem,
    red_sem,
):
    gz_n, gy_n, vec_n, depth, height, rows, width, chunks = sizes
    pairs = vec_n // 2
    lanes = 2 * width
    me_z = lax.axis_index("gz")
    me_y = lax.axis_index("gy")
    me_v = lax.axis_index("vec")
    pair = me_v // 2
    side = lax.rem(me_v, 2)
    group = gz_n * gy_n
    me_g = me_z * gy_n + me_y
    span = depth // chunks

    def member(step):
        return lax.rem(me_g + step, group)

    def place(g):
        return {"gz": g // gy_n, "gy": lax.rem(g, gy_n)}

    barrier = pltpu.get_barrier_semaphore()
    for step in range(1, group):
        pl.semaphore_signal(barrier, inc=1, device_id=place(member(step)), device_id_type=MESH)
    for step in range(1, vec_n):
        pl.semaphore_signal(
            barrier, inc=1, device_id={"vec": lax.rem(me_v + step, vec_n)}, device_id_type=MESH
        )
    centre = ext.at[pl.ds(1, depth), pl.ds(1, height)]
    locals_ = [
        pltpu.make_async_copy(v_ref, centre, local_sem.at[0]),
        pltpu.make_async_copy(v_ref, left.at[pair, side], local_sem.at[1]),
    ]
    scalars = [
        pltpu.make_async_copy(momentum_in, momentum_ref, local_sem.at[2]),
        pltpu.make_async_copy(directions_in, directions_ref, local_sem.at[3]),
    ]
    for copy in scalars + locals_:
        copy.start()
    pl.semaphore_wait(barrier, group - 1 + vec_n - 1)

    counter = [0]

    def remote(src, dst, device):
        index = counter[0]
        counter[0] += 1
        return pltpu.make_async_remote_copy(
            src_ref=src,
            dst_ref=dst,
            send_sem=send_sem.at[index],
            recv_sem=recv_sem.at[index],
            device_id=device,
            device_id_type=MESH,
        )

    z_up = {"gz": lax.rem(me_z + 1, gz_n)}
    z_down = {"gz": lax.rem(me_z + gz_n - 1, gz_n)}
    y_up = {"gy": lax.rem(me_y + 1, gy_n)}
    y_down = {"gy": lax.rem(me_y + gy_n - 1, gy_n)}
    sibling = {"vec": pair * 2 + 1 - side}
    inner_y = pl.ds(1, height)
    z_copies = [
        remote(v_ref.at[depth - 1], ext.at[0, inner_y], z_up),
        remote(v_ref.at[0], ext.at[depth + 1, inner_y], z_down),
        remote(links_far.at[2, depth - 1], rim_z, z_up),
    ]
    rim_copy = remote(links_far.at[1, :, height - 1], rim_y, y_up)
    near = remote(v_ref, left.at[pair, side], sibling)
    far, relay, y_copies = [], [], []
    for k in range(chunks):
        part = pl.ds(k * span, span)
        inner_z = pl.ds(1 + k * span, span)
        y_copies.append(
            (
                remote(v_ref.at[part, height - 1], ext.at[inner_z, 0], y_up),
                remote(v_ref.at[part, 0], ext.at[inner_z, height + 1], y_down),
            )
        )
        for hop in range(1, pairs):
            target = lax.rem(pair + hop, pairs)
            source = lax.rem(pair + pairs - hop, pairs)
            far.append(
                remote(v_ref.at[part], left.at[pair, side, part], {"vec": target * 2 + side})
            )
            relay.append(
                remote(left.at[source, side, part], left.at[source, side, part], sibling)
            )
    rim_copy.start()
    for copy in z_copies:
        copy.start()
    for k in range(chunks):
        for copy in far[k * (pairs - 1) : (k + 1) * (pairs - 1)]:
            copy.start()
        for copy in y_copies[k]:
            copy.start()
    near.start()

    lane = lax.broadcasted_iota(jnp.int32, (1, lanes), 1)
    low_half = lane < width
    last_mask = lax.rem(lane, width) == width - 1
    first_mask = lax.rem(lane, width) == 0
    sign = jnp.where(low_half, 1.0, -1.0).astype(jnp.float32)
    tile = 32 if rows % 32 == 0 else rows

    for copy in scalars:
        copy.wait()
    site_shape = (depth * height, lanes)
    site = lax.broadcasted_iota(jnp.int32, site_shape, 0)
    x_at = lax.rem(lax.broadcasted_iota(jnp.int32, site_shape, 1), width)
    y_at = me_y * height + lax.rem(site, height)
    z_at = me_z * depth + site // height

    def fraction(component, at, extent):
        turned = lax.rem(momentum_ref[component] * at, extent)
        turned = jnp.where(turned < 0, turned + extent, turned)
        return turned.astype(jnp.float32) / extent

    angle = (2.0 * math.pi) * (
        fraction(2, z_at, depth * gz_n)
        + fraction(1, y_at, height * gy_n)
        + fraction(0, x_at, width)
    )
    cos_ref[...] = jnp.cos(angle)
    sin_ref[...] = jnp.sin(angle) * sign

    def coefficients(raw):
        value = raw.astype(jnp.float32) * 0.5
        swapped = pltpu.roll(value, width, 1)
        real = jnp.where(low_half, value, swapped)
        imag = jnp.where(low_half, -swapped, value)
        return real, imag

    def put(table, where, pair_of):
        table[where + (slice(0, 9),)] = pair_of[0]
        table[where + (slice(16, 25),)] = pair_of[1]

    def step_back(value):
        one = pltpu.roll(value, 1, 1)
        two = pltpu.roll(value, width + 1, 1)
        return jnp.where(first_mask, two, one)

    def make_tables(z):
        for y in range(height):
            real, imag = coefficients(links_ref[0, z, y])
            put(tab_x, (0, z, y), (real, imag))
            put(tab_x, (1, z, y), (step_back(real), step_back(imag)))
            put(tab_y, (z, y + 1), coefficients(links_ref[1, z, y]))
            put(tab_z, (z + 1, y), coefficients(links_ref[2, z, y]))

    pl.loop(0, depth)(make_tables)

    def store(z, y, colour, slot, lo, value):
        turned = pltpu.roll(value, width, 1) * sign
        trans[z, y, colour, pl.ds(slot * 2 * rows + lo, tile)] = value.astype(jnp.bfloat16)
        trans[z, y, colour, pl.ds((slot * 2 + 1) * rows + lo, tile)] = turned.astype(jnp.bfloat16)

    def load(z, y, colour, lo):
        return ext[z, y, colour, pl.ds(lo, tile)].astype(jnp.float32)

    def stencil(z, y, lo, slot, ahead, behind, up, down):
        sums = [0.0, 0.0, 0.0]
        for col in range(3):
            value, swapped = ahead(col)
            for row in range(3):
                k = row * 3 + col
                sums[row] = sums[row] + (up(k) * value + up(16 + k) * swapped)
        for col in range(3):
            value, swapped = behind(col)
            for row in range(3):
                k = col * 3 + row
                sums[row] = sums[row] + (down(16 + k) * swapped - down(k) * value)
        for row in range(3):
            store(z, y, row, slot, lo, sums[row])

    def swap(value):
        return value, pltpu.roll(value, width, 1)

    def pass_x(z):
        for y in range(height):
            for lo in range(0, rows, tile):
                here = pl.ds(z * height + y, 1)
                cosine = cos_ref[here]
                sine = sin_ref[here]

                def ahead(col):
                    value = load(z + 1, y + 1, col, lo)
                    one = pltpu.roll(value, lanes - 1, 1)
                    two = pltpu.roll(value, width - 1, 1)
                    return jnp.where(last_mask, two, one), jnp.where(last_mask, one, two)

                def behind(col):
                    value = load(z + 1, y + 1, col, lo)
                    one = pltpu.roll(value, 1, 1)
                    two = pltpu.roll(value, width + 1, 1)
                    return jnp.where(first_mask, two, one), jnp.where(first_mask, one, two)

                stencil(
                    z, y, lo, 0, ahead, behind,
                    lambda k: tab_x[0, z, y, k : k + 1],
                    lambda k: tab_x[1, z, y, k : k + 1],
                )
                for col in range(3):
                    value, swapped = swap(load(z + 1, y + 1, col, lo))
                    store(z, y, col, 2, lo, value * cosine + swapped * sine)

    def pass_y(z):
        for y in range(height):
            for lo in range(0, rows, tile):
                stencil(
                    z, y, lo, 3,
                    lambda col: swap(load(z + 1, y + 2, col, lo)),
                    lambda col: swap(load(z + 1, y, col, lo)),
                    lambda k: tab_y[z, y + 1, k : k + 1],
                    lambda k: tab_y[z, y, k : k + 1],
                )

    def pass_z(z):
        for y in range(height):
            for lo in range(0, rows, tile):
                stencil(
                    z, y, lo, 1,
                    lambda col: swap(load(z + 2, y + 1, col, lo)),
                    lambda col: swap(load(z, y + 1, col, lo)),
                    lambda k: tab_z[z + 1, y, k : k + 1],
                    lambda k: tab_z[z, y, k : k + 1],
                )

    def contract(which, chunk, lo, hi, fresh):
        sites = [
            (chunk * span + dz, y, c) for dz in range(span) for y in range(height) for c in range(3)
        ]
        a = jnp.concatenate([trans[z, y, c, lo:hi] for z, y, c in sites], axis=1)
        b = jnp.concatenate(
            [
                jnp.concatenate([left[which, s, z, y, c] for z, y, c in sites], axis=1)
                for s in range(2)
            ],
            axis=0,
        )
        product = lax.dot_general(
            a, b, (((1,), (1,)), ((), ())), preferred_element_type=jnp.float32
        )
        columns = pl.ds(pl.multiple_of(which * 2 * rows, 2 * rows), 2 * rows)
        if fresh:
            acc[lo:hi, columns] = product
        else:
            acc[lo:hi, columns] += product

    for copy in locals_:
        copy.wait()
    pl.loop(0, depth)(pass_x)
    for copy in z_copies:
        copy.wait()
    for y in range(height):
        put(tab_z, (0, y), coefficients(rim_z[y]))
    pl.loop(0, depth)(pass_z)

    early = 6 * rows
    near.wait()
    contract(pair, 0, 0, early, True)
    pl.loop(1, chunks)(lambda k: contract(pair, k, 0, early, False))

    own_columns = pl.ds(pl.multiple_of(pair * 2 * rows, 2 * rows), 2 * rows)
    stages = [
        [(own_columns, 0, early)],
        [
            (
                pl.ds(
                    pl.multiple_of(lax.rem(pair + pairs - hop, pairs) * 2 * rows, 2 * rows),
                    2 * rows,
                ),
                0,
                8 * rows,
            )
            for hop in range(1, pairs)
        ]
        + [(own_columns, early, 8 * rows)],
    ]

    def exchange(stage, phase, step):
        source = outgo[stage].at[member(step)] if phase == 0 else reduced[stage]
        target = income[stage] if phase == 0 else gathered[stage]
        return pltpu.make_async_remote_copy(
            src_ref=source,
            dst_ref=target.at[me_g],
            send_sem=red_sem.at[stage, phase, 0, step],
            recv_sem=red_sem.at[stage, phase, 1, step],
            device_id=place(member(step)),
            device_id_type=MESH,
        )

    def pieces(stage):
        at = 0
        for columns, lo, hi in stages[stage]:
            share = (hi - lo) // group
            yield columns, lo, share, at
            at += share

    def scatter_start(stage):
        for columns, lo, share, at in pieces(stage):
            for g in range(group):
                outgo[stage][g, at : at + share] = acc[
                    lo + g * share : lo + (g + 1) * share, columns
                ].astype(jnp.bfloat16)
        for step in range(1, group):
            exchange(stage, 0, step).start()

    def gather_start(stage):
        for step in range(1, group):
            exchange(stage, 0, step).wait()
        total = outgo[stage][me_g].astype(jnp.float32)
        for step in range(1, group):
            total = total + income[stage][member(step)].astype(jnp.float32)
        reduced[stage][...] = total.astype(jnp.bfloat16)
        gathered[stage][me_g] = total.astype(jnp.bfloat16)
        for step in range(1, group):
            exchange(stage, 1, step).start()

    def gather_finish(stage):
        for step in range(1, group):
            exchange(stage, 1, step).wait()
        for columns, lo, share, at in pieces(stage):
            for g in range(group):
                acc[lo + g * share : lo + (g + 1) * share, columns] = gathered[stage][
                    g, at : at + share
                ].astype(jnp.float32)

    scatter_start(0)
    rim_copy.wait()

    @pl.loop(0, depth)
    def _(z):
        put(tab_y, (z, 0), coefficients(rim_y[z]))

    for k in range(chunks + 1):
        if k < chunks:
            for hop in range(1, pairs):
                index = k * (pairs - 1) + hop - 1
                far[index].wait()
                relay[index].start()
            for copy in y_copies[k]:
                copy.wait()
            pl.loop(k * span, (k + 1) * span)(pass_y)
            contract(pair, k, early, 8 * rows, k == 0)
        if k == chunks - 1:
            gather_start(0)
        if k:
            for hop in range(1, pairs):
                relay[(k - 1) * (pairs - 1) + hop - 1].wait()
                contract(lax.rem(pair + pairs - hop, pairs), k - 1, 0, 8 * rows, k == 1)

    scatter_start(1)
    gather_start(1)
    gather_finish(0)
    gather_finish(1)

    scale = 1.0 / math.sqrt(width * height * gy_n * depth * gz_n)
    full = acc[...] * scale
    along_x, along_z, phased, along_y = [
        full[slot * 2 * rows : (slot + 1) * 2 * rows] for slot in range(4)
    ]
    for slot in range(3):
        chosen = directions_ref[slot]
        out_ref[slot * 2 * rows : (slot + 1) * 2 * rows] = jnp.where(
            chosen == 0, along_x, jnp.where(chosen == 1, along_y, along_z)
        )
    out_ref[6 * rows :] = phased


def body(vectors, links, momentum, directions):
    rows, _, depth, height, lanes = vectors.shape
    gz_n = lax.axis_size("gz")
    gy_n = lax.axis_size("gy")
    vec_n = lax.axis_size("vec")
    group = gz_n * gy_n
    chunks = split_chunks(depth, 4)
    v = jnp.transpose(vectors, (2, 3, 1, 0, 4))
    packed = jnp.transpose(links, (0, 3, 4, 1, 2, 5)).reshape(3, depth, height, 9, lanes)

    bf16, f32 = jnp.bfloat16, jnp.float32
    pairs = vec_n // 2
    shares = (6 * rows // group, (8 * (pairs - 1) + 2) * rows // group)
    remote_count = 5 + chunks * (2 + 2 * (pairs - 1))
    vmem = pl.BlockSpec(memory_space=pltpu.VMEM)
    hbm = pl.BlockSpec(memory_space=pl.ANY)
    sizes = (gz_n, gy_n, vec_n, depth, height, rows, lanes // 2, chunks)
    out = pl.pallas_call(
        functools.partial(kernel, sizes),
        out_shape=jax.ShapeDtypeStruct((8 * rows, vec_n * rows), f32),
        in_specs=[hbm, hbm, hbm, vmem, hbm],
        out_specs=vmem,
        scratch_shapes=[
            pltpu.VMEM((depth + 2, height + 2, 3, rows, lanes), bf16),
            pltpu.VMEM((pairs, 2, depth, height, 3, rows, lanes), bf16),
            pltpu.VMEM((depth, 9, lanes), bf16),
            pltpu.VMEM((height, 9, lanes), bf16),
            pltpu.VMEM((2, depth, height, 32, lanes), f32),
            pltpu.VMEM((depth, height + 1, 32, lanes), f32),
            pltpu.VMEM((depth + 1, height, 32, lanes), f32),
            pltpu.VMEM((depth * height, lanes), f32),
            pltpu.VMEM((depth * height, lanes), f32),
            pltpu.VMEM((depth, height, 3, 8 * rows, lanes), bf16),
            pltpu.VMEM((8 * rows, vec_n * rows), f32),
            pltpu.SMEM((3,), jnp.int32),
            pltpu.SMEM((3,), jnp.int32),
            [pltpu.VMEM((group, share, 2 * rows), bf16) for share in shares],
            [pltpu.VMEM((group, share, 2 * rows), bf16) for share in shares],
            [pltpu.VMEM((share, 2 * rows), bf16) for share in shares],
            [pltpu.VMEM((group, share, 2 * rows), bf16) for share in shares],
            pltpu.SemaphoreType.DMA((4,)),
            pltpu.SemaphoreType.DMA((remote_count,)),
            pltpu.SemaphoreType.DMA((remote_count,)),
            pltpu.SemaphoreType.DMA((2, 2, 2, group)),
        ],
        compiler_params=pltpu.CompilerParams(
            collective_id=0, has_side_effects=True, vmem_limit_bytes=48 * 1024 * 1024
        ),
    )(momentum, directions, v, packed, packed)
    return out.reshape(4, 2, rows, vec_n * rows)


def solution(mesh):
    in_specs = (P("vec", None, "gz", "gy", None), P(None, None, None, "gz", "gy", None), P(), P())
    out_specs = P(None, None, "vec", None)
    return jax.shard_map(body, mesh=mesh, in_specs=in_specs, out_specs=out_specs, check_vma=False)
```

profile of v0, /device:TPU:0, one launch (start us, length us, event | category | flops | bytes accessed | tf_op | source)
XLA Modules:
  0.0 43.6 jit_solution(17235026366733200226)
XLA Ops:
  0.0 0.9 %copy.8 = bf16[3,3,3,8,2,128]{5,3,2,1,4,0:T(8,128)(2,1)S(1)} copy(bf16[3,3,3,8,2,128]{5,4,3,2,1,0:T(2,128)(2,1)} %param.5) | data formatting | bytes 221184 | tf_op args[1]
  1.0 1.3 %copy.12 = bf16[64,3,8,2,128]{4,0,1,3,2:T(8,128)(2,1)S(1)} copy(bf16[64,3,8,2,128]{4,3,2,1,0:T(2,128)(2,1)} %param.4) | data formatting | bytes 1572864 | tf_op args[0]
  2.3 0.0 copy-start
  2.3 0.0 copy-start.1
  2.3 0.6 %copy-done = s32[3]{0:T(128)S(1)} copy-done((s32[3]{0:T(128)S(1)}, s32[3]{0:T(128)}, u32[]{:S(2)}) %copy-start) | copy-done | bytes 36
  3.0 0.0 copy-done.1
  3.0 39.8 %shard_map.46 = f32[512,256]{1,0:T(8,128)S(1)} custom-call(s32[3]{0:T(128)S(1)} %copy-done, s32[3]{0:T(128)S(1)} %copy-done.1, bf16[8,2,3,64,128]{4,3,2,1,0:T(8,128)(2,1)S(1)} %bitcast.7, bf16[3,8,2,9,128]{4,3,2,1,0:T(8,128)(2,1)S(1)} %copy.9.links_ref.links_far, bf16[3,8,2,9,128]{4,3,2,1,0:T(8,128)(2,1)S(1)} %copy.9.links_ref.links_far), custom_call_target="tpu_custom_call" | custom-call | tf_op jit(solution)/shard_map/pallas_call | solution.py:434
  42.8 0.8 %copy.14 = f32[4,2,64,256]{3,2,1,0:T(8,128)} copy(f32[4,2,64,256]{3,2,1,0:T(8,128)S(1)} %bitcast.8) | data formatting | bytes 1048576
  (1 shorter events, 0.0 us)
Async XLA Ops:
  2.3 0.7 %copy-start = (s32[3]{0:T(128)S(1)}, s32[3]{0:T(128)}, u32[]{:S(2)}) copy-start(s32[3]{0:T(128)} %momentum_in.1) | copy-start | bytes 40
  2.3 0.7 %copy-start.1 = (s32[3]{0:T(128)S(1)}, s32[3]{0:T(128)}, u32[]{:S(2)}) copy-start(s32[3]{0:T(128)} %directions_in.1) | copy-start | bytes 40
where the time goes:
time: 43.7 us; the launch traced here: 43.6 us
  Pallas kernels  39.8 us (91%)
  local copies, waits for them, and re-layouts  3.74 us (9%)
    pallas_call x1, Pallas kernels, body(): pl.pallas_call(functools.partial(kernel, sizes), out_shape=jax.ShapeDtype...  39.8 us
    unnamed x7, local copies, waits for them, and re-layouts  3.7 us

commit v1 on v0

v1 whole, which is shorter than its diff:
```python
import functools
import math

import jax
import jax.numpy as jnp
from jax import lax
from jax.experimental import pallas as pl
from jax.experimental.pallas import tpu as pltpu
from jax.sharding import PartitionSpec as P

MESH = pl.DeviceIdType.MESH


def split_chunks(depth, most):
    count = most
    while depth % count or (depth // count) % 2:
        count -= 1
    return count


def kernel(
    sizes,
    momentum_in,
    directions_in,
    v_ref,
    links_ref,
    out_ref,
    left,
    halo_y,
    halo_z,
    rim_y,
    rim_z,
    tab_x,
    tab_y,
    tab_z,
    edge_y,
    edge_z,
    cos_ref,
    sin_ref,
    trans_a,
    trans_b,
    acc,
    momentum_ref,
    directions_ref,
    outgo,
    income,
    reduced,
    gathered,
    cross_out,
    cross_in,
    back_out,
    back_in,
    local_sem,
    send_sem,
    recv_sem,
    red_sem,
    cross_sem,
):
    gz_n, gy_n, vec_n, depth, height, rows, width, chunks = sizes
    lanes = 2 * width
    two = 2 * rows
    me_z = lax.axis_index("gz")
    me_y = lax.axis_index("gy")
    me_v = lax.axis_index("vec")
    pair = me_v // 2
    side = lax.rem(me_v, 2)
    group = gz_n * gy_n
    me_g = me_z * gy_n + me_y
    span = depth // chunks
    share = rows // group
    partners = [me_v, pair * 2 + 1 - side, (1 - pair) * 2 + side, (1 - pair) * 2 + 1 - side]

    def member(step):
        return lax.rem(me_g + step, group)

    def place(g, k=0):
        return {"gz": g // gy_n, "gy": lax.rem(g, gy_n), "vec": partners[k]}

    barrier = pltpu.get_barrier_semaphore()
    for k in range(vec_n):
        for step in range(group):
            if k or step:
                pl.semaphore_signal(
                    barrier, inc=1, device_id=place(member(step), k), device_id_type=MESH
                )
    scalars = [
        pltpu.make_async_copy(momentum_in, momentum_ref, local_sem.at[0]),
        pltpu.make_async_copy(directions_in, directions_ref, local_sem.at[1]),
    ]
    for copy in scalars:
        copy.start()

    lane = lax.broadcasted_iota(jnp.int32, (1, lanes), 1)
    low_half = lane < width
    last_mask = lax.rem(lane, width) == width - 1
    first_mask = lax.rem(lane, width) == 0
    sign = jnp.where(low_half, 1.0, -1.0).astype(jnp.float32)
    tile = 32 if rows % 32 == 0 else rows

    def coefficients(raw):
        value = raw.astype(jnp.float32) * 0.5
        swapped = pltpu.roll(value, width, 1)
        real = jnp.where(low_half, value, swapped)
        imag = jnp.where(low_half, -swapped, value)
        return real, imag

    def put(table, where, pair_of):
        table[where + (slice(0, 9),)] = pair_of[0]
        table[where + (slice(16, 25),)] = pair_of[1]

    def step_back(value):
        one = pltpu.roll(value, 1, 1)
        other = pltpu.roll(value, width + 1, 1)
        return jnp.where(first_mask, other, one)

    @pl.loop(0, depth)
    def _(z):
        for y in range(height):
            real, imag = coefficients(links_ref[0, z, y])
            put(tab_x, (0, z, y), (real, imag))
            put(tab_x, (1, z, y), (step_back(real), step_back(imag)))
            put(tab_y, (z, y), coefficients(links_ref[1, z, y]))
            put(tab_z, (z, y), coefficients(links_ref[2, z, y]))

    for copy in scalars:
        copy.wait()
    site_shape = (depth * height, lanes)
    site = lax.broadcasted_iota(jnp.int32, site_shape, 0)
    x_at = lax.rem(lax.broadcasted_iota(jnp.int32, site_shape, 1), width)
    y_at = me_y * height + lax.rem(site, height)
    z_at = me_z * depth + site // height

    def fraction(component, at, extent):
        turned = lax.rem(momentum_ref[component] * at, extent)
        turned = jnp.where(turned < 0, turned + extent, turned)
        return turned.astype(jnp.float32) / extent

    angle = (2.0 * math.pi) * (
        fraction(2, z_at, depth * gz_n)
        + fraction(1, y_at, height * gy_n)
        + fraction(0, x_at, width)
    )
    cos_ref[...] = jnp.cos(angle)
    sin_ref[...] = jnp.sin(angle) * sign

    pl.semaphore_wait(barrier, group * vec_n - 1)

    counter = [0]

    def remote(src, dst, device):
        index = counter[0]
        counter[0] += 1
        return pltpu.make_async_remote_copy(
            src_ref=src,
            dst_ref=dst,
            send_sem=send_sem.at[index],
            recv_sem=recv_sem.at[index],
            device_id=device,
            device_id_type=MESH,
        )

    z_up = {"gz": lax.rem(me_z + 1, gz_n)}
    z_down = {"gz": lax.rem(me_z + gz_n - 1, gz_n)}
    y_up = {"gy": lax.rem(me_y + 1, gy_n)}
    y_down = {"gy": lax.rem(me_y + gy_n - 1, gy_n)}
    sibling = {"vec": partners[1]}
    rim_y_copy = remote(links_ref.at[1, :, height - 1], rim_y, y_up)
    rim_z_copy = remote(links_ref.at[2, depth - 1], rim_z, z_up)
    z_copies = [
        remote(v_ref.at[depth - 1 if y % 2 else 0, y], halo_z.at[y], z_up if y % 2 else z_down)
        for y in range(height)
    ]
    y_copies = [
        remote(v_ref.at[z, height - 1 if z % 2 else 0], halo_y.at[z], y_up if z % 2 else y_down)
        for z in range(depth)
    ]
    near = remote(v_ref, left.at[0], sibling)
    far, relay = [], []
    for k in range(chunks):
        part = pl.ds(k * span, span)
        far.append(remote(v_ref.at[part], left.at[1, part], {"vec": partners[2]}))
        relay.append(remote(left.at[1, part], left.at[2, part], sibling))
    far[0].start()
    rim_y_copy.start()
    rim_z_copy.start()
    for copy in z_copies:
        copy.start()
    for copy in y_copies + far[1:]:
        copy.start()
    near.start()

    def store(ref, where, slot, lo, value):
        turned = pltpu.roll(value, width, 1) * sign
        ref[where + (pl.ds(slot * two + lo, tile),)] = value.astype(jnp.bfloat16)
        ref[where + (pl.ds(slot * two + rows + lo, tile),)] = turned.astype(jnp.bfloat16)

    def load(z, y, colour, lo):
        return v_ref[z, y, colour, pl.ds(lo, tile)].astype(jnp.float32)

    def stencil(ref, where, lo, slot, ahead, behind, up, down):
        sums = [0.0, 0.0, 0.0]
        for col in range(3):
            value, swapped = ahead(col)
            for row in range(3):
                k = row * 3 + col
                sums[row] = sums[row] + (up(k) * value + up(16 + k) * swapped)
        for col in range(3):
            value, swapped = behind(col)
            for row in range(3):
                k = col * 3 + row
                sums[row] = sums[row] + (down(16 + k) * swapped - down(k) * value)
        for row in range(3):
            store(ref, where + (row,), slot, lo, sums[row])

    def swap(value):
        return value, pltpu.roll(value, width, 1)

    def pass_x(z):
        for y in range(height):
            for lo in range(0, rows, tile):
                here = pl.ds(z * height + y, 1)
                cosine = cos_ref[here]
                sine = sin_ref[here]

                def ahead(col):
                    value = load(z, y, col, lo)
                    one = pltpu.roll(value, lanes - 1, 1)
                    other = pltpu.roll(value, width - 1, 1)
                    return jnp.where(last_mask, other, one), jnp.where(last_mask, one, other)

                def behind(col):
                    value = load(z, y, col, lo)
                    one = pltpu.roll(value, 1, 1)
                    other = pltpu.roll(value, width + 1, 1)
                    return jnp.where(first_mask, other, one), jnp.where(first_mask, one, other)

                stencil(
                    trans_a, (z, y), lo, 0, ahead, behind,
                    lambda k: tab_x[0, z, y, k : k + 1],
                    lambda k: tab_x[1, z, y, k : k + 1],
                )
                for col in range(3):
                    value, swapped = swap(load(z, y, col, lo))
                    store(trans_a, (z, y, col), 1, lo, value * cosine + swapped * sine)

    def halo(ref, at):
        return lambda col, lo: ref[at, col, pl.ds(lo, tile)].astype(jnp.float32)

    def inside(z, y):
        return lambda col, lo: load(z, y, col, lo)

    def derive(z, y, slot, ahead, behind, up, down):
        for lo in range(0, rows, tile):
            stencil(
                trans_b, (z, y // 2), lo, slot,
                lambda col: swap(ahead(col, lo)),
                lambda col: swap(behind(col, lo)),
                up,
                down,
            )

    def table(ref, where):
        return lambda k: ref[where + (slice(k, k + 1),)]

    def derive_z(z, y, ahead=None, behind=None, down=None):
        derive(
            z, y, 0,
            ahead or inside(z + 1, y),
            behind or inside(z - 1, y),
            table(tab_z, (z, y)),
            down or table(tab_z, (z - 1, y)),
        )

    def derive_y(z, y):
        top, bottom = y == height - 1, y == 0
        derive(
            z, y, 1,
            halo(halo_y, z) if top else inside(z, y + 1),
            halo(halo_y, z) if bottom else inside(z, y - 1),
            table(tab_y, (z, y)),
            table(edge_y, (z,)) if bottom else table(tab_y, (z, y - 1)),
        )

    def pass_z(t):
        for y in range(0, height, 2):
            derive_z(2 * t + 1, y)
        for y in range(1, height, 2):
            derive_z(2 * t + 2, y)

    def pass_z_edges():
        for y in range(1, height, 2):
            derive_z(0, y, behind=halo(halo_z, y), down=table(edge_z, (y,)))
        for y in range(0, height, 2):
            derive_z(depth - 1, y, ahead=halo(halo_z, y))

    def pass_y(t):
        for dz in range(2):
            for y in range(1 - dz, height, 2):
                derive_y(2 * t + dz, y)

    def pick(k):
        return v_ref if k == 0 else left.at[k - 1]

    def contract(outer, chunk, ref, lo, hi, base, fresh):
        sites = [
            (chunk * span + dz, y, c)
            for dz in range(span)
            for y in (range(height) if ref is trans_a else range(1 - dz % 2, height, 2))
            for c in range(3)
        ]
        a = jnp.concatenate(
            [ref[z, y if ref is trans_a else y // 2, c, lo:hi] for z, y, c in sites], axis=1
        )
        b = jnp.concatenate(
            [
                jnp.concatenate([pick(outer * 2 + s)[z, y, c] for z, y, c in sites], axis=1)
                for s in range(2)
            ],
            axis=0,
        )
        product = lax.dot_general(
            a, b, (((1,), (1,)), ((), ())), preferred_element_type=jnp.float32
        )
        columns = slice(outer * two, (outer + 1) * two)
        if fresh:
            acc[base + lo : base + hi, columns] = product
        else:
            acc[base + lo : base + hi, columns] += product

    half = 4 * rows

    def contract_all(outer, ref, lo, hi, base):
        contract(outer, 0, ref, lo, hi, base, True)
        pl.loop(1, chunks)(lambda k: contract(outer, k, ref, lo, hi, base, False))

    pl.loop(0, depth)(pass_x)
    far[0].wait()
    relay[0].start()
    pl.loop(0, depth // 2 - 1)(pass_z)
    for copy in z_copies:
        copy.wait()
    rim_z_copy.wait()
    for y in range(1, height, 2):
        put(edge_z, (y,), coefficients(rim_z[y]))
    pass_z_edges()
    near.wait()
    contract_all(0, trans_a, 0, half, 0)
    contract_all(0, trans_b, 0, two, half)
    rim_y_copy.wait()

    @pl.loop(0, depth // 2)
    def _(t):
        put(edge_y, (2 * t + 1,), coefficients(rim_y[2 * t + 1]))

    for copy in y_copies:
        copy.wait()
    pl.loop(0, depth // 2)(pass_y)
    contract_all(0, trans_b, two, half, half)

    left_half = lax.broadcasted_iota(jnp.int32, (1, two), 1) < rows
    kept_near, kept_far = side, pair

    def turn(value):
        return pltpu.roll(value, rows, 1)

    def exchange(stage, phase, step):
        source = outgo[stage].at[member(step)] if phase == 0 else reduced[stage]
        target = income[stage] if phase == 0 else gathered[stage]
        return pltpu.make_async_remote_copy(
            src_ref=source,
            dst_ref=target.at[me_g],
            send_sem=red_sem.at[stage, phase, 0, step],
            recv_sem=red_sem.at[stage, phase, 1, step],
            device_id=place(member(step)),
            device_id_type=MESH,
        )

    def cross(k, phase, step):
        source = cross_out.at[k - 1, member(step)] if phase == 0 else back_out.at[k - 1]
        target = cross_in if phase == 0 else back_in
        return pltpu.make_async_remote_copy(
            src_ref=source,
            dst_ref=target.at[k - 1, me_g],
            send_sem=cross_sem.at[k - 1, phase, 0, step],
            recv_sem=cross_sem.at[k - 1, phase, 1, step],
            device_id=place(member(step), k),
            device_id_type=MESH,
        )

    stage_partners = [(1,), (2, 3)]
    stage_rows = [
        [slot * rows for slot in range(8)],
        [slot * rows for slot in (0, 1, 2, 3, 4, 6)],
    ]

    def prepare(stage):
        columns = slice(stage * two, (stage + 1) * two)
        sent = []
        for op in range(2):
            base = half + op * two
            block = acc[base : base + two, columns]
            turned = jnp.transpose(block)
            if stage == 0:
                own = turned[0:rows]
                acc[base : base + rows, columns] = block[0:rows] - jnp.where(left_half, own, 0.0)
                acc[base + rows : base + two, columns] = block[rows:two] + jnp.where(
                    left_half, turn(own), 0.0
                )
                sent.append([turned[rows:two]])
            else:
                acc[base : base + rows, columns] = jnp.where(
                    kept_far == 0, block[0:rows], block[rows:two]
                )
                sent.append([turned[0:rows], turned[rows:two]])
        kept = kept_near if stage == 0 else kept_far
        for at, k in enumerate(stage_partners[stage]):
            first, second = sent[0][at], sent[1][at]
            if_real = jnp.where(left_half, -first, -turn(second))
            if_imag = jnp.where(left_half, turn(first), second)
            message = jnp.where(kept == 1, if_real, if_imag).astype(jnp.bfloat16)
            for g in range(group):
                cross_out[k - 1, g] = message[g * share : (g + 1) * share]

    def scatter_start(stage):
        columns = slice(stage * two, (stage + 1) * two)
        prepare(stage)
        for g in range(group):
            for at, row in enumerate(stage_rows[stage]):
                outgo[stage][g, at * share : (at + 1) * share] = acc[
                    row + g * share : row + (g + 1) * share, columns
                ].astype(jnp.bfloat16)
        for step in range(1, group):
            exchange(stage, 0, step).start()
        for k in stage_partners[stage]:
            for step in range(group):
                cross(k, 0, step).start()

    def gather_start(stage):
        columns = slice(stage * two, (stage + 1) * two)
        for step in range(1, group):
            exchange(stage, 0, step).wait()
        for k in stage_partners[stage]:
            for step in range(group):
                cross(k, 0, step).wait()
        parts = []
        for at, row in enumerate(stage_rows[stage]):
            if share % 8 == 0:
                mine = pl.ds(pl.multiple_of(row + me_g * share, share), share)
                total = acc[mine, columns]
            else:
                total = outgo[stage][me_g, at * share : (at + 1) * share].astype(jnp.float32)
            for step in range(1, group):
                total = total + income[stage][
                    member(step), at * share : (at + 1) * share
                ].astype(jnp.float32)
            parts.append(total)
        extra = []
        for k in stage_partners[stage]:
            total = cross_in[k - 1, 0].astype(jnp.float32)
            for g in range(1, group):
                total = total + cross_in[k - 1, g].astype(jnp.float32)
            extra.append(total)
        if stage == 0:
            adds = [turn(extra[0]), extra[0]]
            for op in range(2):
                add = jnp.where(left_half, 0.0, adds[op])
                for part in range(2):
                    at = 4 + op * 2 + part
                    parts[at] = parts[at] + jnp.where(kept_near == part, add, 0.0)
            kept_of = [
                jnp.where(kept_near == 0, parts[4 + op * 2], parts[5 + op * 2]) for op in range(2)
            ]
            backs = [jnp.where(left_half, turn(kept_of[0]), kept_of[1])]
        else:
            parts[4] = parts[4] + jnp.where(left_half, extra[0], turn(extra[1]))
            parts[5] = parts[5] + jnp.where(left_half, turn(extra[0]), extra[1])
            backs = [
                jnp.where(left_half, parts[4], turn(parts[5])),
                jnp.where(left_half, turn(parts[4]), parts[5]),
            ]
        for at, total in enumerate(parts):
            rounded = total.astype(jnp.bfloat16)
            reduced[stage][at * share : (at + 1) * share] = rounded
            gathered[stage][me_g, at * share : (at + 1) * share] = rounded
        for k, back in zip(stage_partners[stage], backs):
            back_out[k - 1] = back.astype(jnp.bfloat16)
        for step in range(1, group):
            exchange(stage, 1, step).start()
        for k in stage_partners[stage]:
            for step in range(group):
                cross(k, 1, step).start()

    scale = 1.0 / math.sqrt(width * height * gy_n * depth * gz_n)

    def gather_finish(stage):
        for step in range(1, group):
            exchange(stage, 1, step).wait()
        for k in stage_partners[stage]:
            for step in range(group):
                cross(k, 1, step).wait()

        def slot(at):
            return jnp.concatenate(
                [
                    gathered[stage][g, at * share : (at + 1) * share].astype(jnp.float32)
                    for g in range(group)
                ],
                axis=0,
            )

        ks = stage_partners[stage]
        mirror = jnp.transpose(
            jnp.concatenate(
                [
                    back_in[k - 1, g].astype(jnp.float32)
                    for k in (ks if len(ks) == 2 else ks * 2)
                    for g in range(group)
                ],
                axis=0,
            )
        )
        full = [slot(at) for at in range(4)]
        for op in range(2):
            flipped = mirror[op * rows : (op + 1) * rows]
            for part in range(2):
                other = -flipped if part == 0 else flipped
                if stage == 0:
                    mine = slot(4 + op * 2 + part)
                    full.append(
                        jnp.where(left_half, mine, jnp.where(kept_near == part, mine, other))
                    )
                else:
                    full.append(jnp.where(kept_far == part, slot(4 + op), other))
        full = [jnp.where(side == 0, value, turn(value)) * scale for value in full]
        which = pair if stage == 0 else 1 - pair
        columns = pl.ds(pl.multiple_of(which * two, two), two)
        for part in range(2):
            along_x, phased, along_z, along_y = [full[2 * op + part] for op in range(4)]
            for op in range(3):
                chosen = directions_ref[op]
                out_ref[op * two + part * rows : op * two + (part + 1) * rows, columns] = jnp.where(
                    chosen == 0, along_x, jnp.where(chosen == 1, along_y, along_z)
                )
            out_ref[3 * two + part * rows : 3 * two + (part + 1) * rows, columns] = phased

    scatter_start(0)
    for k in range(chunks + 1):
        if 0 < k < chunks:
            far[k].wait()
            relay[k].start()
        if k == 2:
            gather_start(0)
        if k:
            relay[k - 1].wait()
            contract(1, k - 1, trans_a, 0, half, 0, k == 1)
            contract(1, k - 1, trans_b, 0, half, half, k == 1)
    scatter_start(1)
    gather_finish(0)
    gather_start(1)
    gather_finish(1)


def body(vectors, links, momentum, directions):
    rows, _, depth, height, lanes = vectors.shape
    gz_n = lax.axis_size("gz")
    gy_n = lax.axis_size("gy")
    vec_n = lax.axis_size("vec")
    group = gz_n * gy_n
    assert vec_n == 4 and depth % 2 == 0 and height % 2 == 0 and rows % group == 0
    chunks = split_chunks(depth, 4)
    v = jnp.transpose(vectors, (2, 3, 1, 0, 4))
    packed = jnp.transpose(links, (0, 3, 4, 1, 2, 5)).reshape(3, depth, height, 9, lanes)

    bf16, f32 = jnp.bfloat16, jnp.float32
    share = rows // group
    slots = (8, 6)
    remote_count = 3 + depth + height + 2 * chunks
    vmem = pl.BlockSpec(memory_space=pltpu.VMEM)
    hbm = pl.BlockSpec(memory_space=pltpu.HBM)
    sizes = (gz_n, gy_n, vec_n, depth, height, rows, lanes // 2, chunks)
    parts = [pltpu.VMEM((group, n * share, 2 * rows), bf16) for n in slots]
    small = pltpu.VMEM((3, group, share, 2 * rows), bf16)
    out = pl.pallas_call(
        functools.partial(kernel, sizes),
        out_shape=jax.ShapeDtypeStruct((8 * rows, vec_n * rows), f32),
        in_specs=[hbm, hbm, vmem, vmem],
        out_specs=vmem,
        scratch_shapes=[
            pltpu.VMEM((3, depth, height, 3, rows, lanes), bf16),
            pltpu.VMEM((depth, 3, rows, lanes), bf16),
            pltpu.VMEM((height, 3, rows, lanes), bf16),
            pltpu.VMEM((depth, 9, lanes), bf16),
            pltpu.VMEM((height, 9, lanes), bf16),
            pltpu.VMEM((2, depth, height, 32, lanes), f32),
            pltpu.VMEM((depth, height, 32, lanes), f32),
            pltpu.VMEM((depth, height, 32, lanes), f32),
            pltpu.VMEM((depth, 32, lanes), f32),
            pltpu.VMEM((height, 32, lanes), f32),
            pltpu.VMEM((depth * height, lanes), f32),
            pltpu.VMEM((depth * height, lanes), f32),
            pltpu.VMEM((depth, height, 3, 4 * rows, lanes), bf16),
            pltpu.VMEM((depth, height // 2, 3, 4 * rows, lanes), bf16),
            pltpu.VMEM((8 * rows, vec_n * rows), f32),
            pltpu.SMEM((3,), jnp.int32),
            pltpu.SMEM((3,), jnp.int32),
            parts,
            parts,
            [pltpu.VMEM((n * share, 2 * rows), bf16) for n in slots],
            parts,
            small,
            small,
            pltpu.VMEM((3, share, 2 * rows), bf16),
            small,
            pltpu.SemaphoreType.DMA((2,)),
            pltpu.SemaphoreType.DMA((remote_count,)),
            pltpu.SemaphoreType.DMA((remote_count,)),
            pltpu.SemaphoreType.DMA((2, 2, 2, group)),
            pltpu.SemaphoreType.DMA((3, 2, 2, group)),
        ],
        compiler_params=pltpu.CompilerParams(
            collective_id=0, has_side_effects=True, vmem_limit_bytes=48 * 1024 * 1024
        ),
    )(momentum, directions, v, packed)
    return out.reshape(4, 2, rows, vec_n * rows)


def solution(mesh):
    in_specs = (P("vec", None, "gz", "gy", None), P(None, None, None, "gz", "gy", None), P(), P())
    out_specs = P(None, None, "vec", None)
    return jax.shard_map(body, mesh=mesh, in_specs=in_specs, out_specs=out_specs, check_vma=False)
```

time: 43.7 us -> 46.8 us (1.071)
  Pallas kernels: 39.8 us -> 42.9 us
    pallas_call x1, Pallas kernels: 39.8 us -> 42.9 us  [body(): pl.pallas_call(functools.partial(kernel, sizes), out_shape=jax.ShapeDtype...]
where the time goes in v1:
time: 46.8 us; the launch traced here: 46.6 us
  Pallas kernels  42.9 us (92%)
  local copies, waits for them, and re-layouts  3.74 us (8%)
    pallas_call x1, Pallas kernels, body(): pl.pallas_call(functools.partial(kernel, sizes), out_shape=jax.ShapeDtype...  42.9 us
    unnamed x7, local copies, waits for them, and re-layouts  3.7 us

profile of v1, /device:TPU:0, one launch (start us, length us, event | category | flops | bytes accessed | tf_op | source)
XLA Modules:
  0.0 46.6 jit_solution(17799092013294531588)
XLA Ops:
  0.0 0.9 %copy.8 = bf16[3,3,3,8,2,128]{5,3,2,1,4,0:T(8,128)(2,1)S(1)} copy(bf16[3,3,3,8,2,128]{5,4,3,2,1,0:T(2,128)(2,1)} %param.5) | data formatting | bytes 221184 | tf_op args[1]
  1.0 1.3 %copy.11 = bf16[64,3,8,2,128]{4,0,1,3,2:T(8,128)(2,1)S(1)} copy(bf16[64,3,8,2,128]{4,3,2,1,0:T(2,128)(2,1)} %param.4) | data formatting | bytes 1572864 | tf_op args[0]
  2.3 0.0 copy-start
  2.3 0.0 copy-start.1
  2.3 0.6 %copy-done = s32[3]{0:T(128)S(1)} copy-done((s32[3]{0:T(128)S(1)}, s32[3]{0:T(128)}, u32[]{:S(2)}) %copy-start) | copy-done | bytes 36
  3.0 0.0 copy-done.1
  3.0 42.9 %shard_map.46 = f32[512,256]{1,0:T(8,128)S(1)} custom-call(s32[3]{0:T(128)S(1)} %copy-done, s32[3]{0:T(128)S(1)} %copy-done.1, bf16[8,2,3,64,128]{4,3,2,1,0:T(8,128)(2,1)S(1)} %bitcast.7, bf16[3,8,2,9,128]{4,3,2,1,0:T(8,128)(2,1)S(1)} %copy.9.links_ref), custom_call_target="tpu_custom_call" | custom-call | tf_op jit(solution)/shard_map/pallas_call | solution.py:583
  45.9 0.8 %copy.13 = f32[4,2,64,256]{3,2,1,0:T(8,128)} copy(f32[4,2,64,256]{3,2,1,0:T(8,128)S(1)} %bitcast.8) | data formatting | bytes 1048576
  (1 shorter events, 0.0 us)
Async XLA Ops:
  2.3 0.7 %copy-start = (s32[3]{0:T(128)S(1)}, s32[3]{0:T(128)}, u32[]{:S(2)}) copy-start(s32[3]{0:T(128)} %momentum_in.1) | copy-start | bytes 40
  2.3 0.7 %copy-start.1 = (s32[3]{0:T(128)S(1)}, s32[3]{0:T(128)}, u32[]{:S(2)}) copy-start(s32[3]{0:T(128)} %directions_in.1) | copy-start | bytes 40

commit v2 on v1

--- a/solution.py
+++ b/solution.py
@@ -55,6 +55,7 @@
     recv_sem,
     red_sem,
     cross_sem,
+    greet_sem,
 ):
     gz_n, gy_n, vec_n, depth, height, rows, width, chunks = sizes
     lanes = 2 * width
@@ -76,13 +77,42 @@
     def place(g, k=0):
         return {"gz": g // gy_n, "gy": lax.rem(g, gy_n), "vec": partners[k]}
 
+    z_up = {"gz": lax.rem(me_z + 1, gz_n)}
+    z_down = {"gz": lax.rem(me_z + gz_n - 1, gz_n)}
+    y_up = {"gy": lax.rem(me_y + 1, gy_n)}
+    y_down = {"gy": lax.rem(me_y + gy_n - 1, gy_n)}
+    sibling = {"vec": partners[1]}
+    across = {"vec": partners[2]}
+    y_sides = [y_up] if gy_n == 2 else [y_up, y_down]
+
+    def tell(sem, device):
+        pl.semaphore_signal(sem, inc=1, device_id=device, device_id_type=MESH)
+
+    def tell_z(sem):
+        pl.when(me_z > 0)(lambda: tell(sem, z_down))
+        pl.when(me_z < gz_n - 1)(lambda: tell(sem, z_up))
+
+    z_sides = jnp.where(me_z > 0, 1, 0) + jnp.where(me_z < gz_n - 1, 1, 0)
     barrier = pltpu.get_barrier_semaphore()
-    for k in range(vec_n):
-        for step in range(group):
-            if k or step:
-                pl.semaphore_signal(
-                    barrier, inc=1, device_id=place(member(step), k), device_id_type=MESH
-                )
+    for device in [sibling, across] + y_sides:
+        tell(barrier, device)
+    tell_z(barrier)
+
+    def greet(number):
+        sem = greet_sem.at[number]
+        if number == 0:
+            tell(sem, sibling)
+        elif number <= gy_n // 2:
+            for device in y_sides:
+                tell(sem, device)
+        else:
+            tell_z(sem)
+
+    def heard(number):
+        sides = 1 if number == 0 else len(y_sides) if number <= gy_n // 2 else z_sides
+        pl.semaphore_wait(greet_sem.at[number], sides)
+
+    rounds = gy_n // 2 + gz_n
     scalars = [
         pltpu.make_async_copy(momentum_in, momentum_ref, local_sem.at[0]),
         pltpu.make_async_copy(directions_in, directions_ref, local_sem.at[1]),
@@ -143,7 +173,7 @@
     cos_ref[...] = jnp.cos(angle)
     sin_ref[...] = jnp.sin(angle) * sign
 
-    pl.semaphore_wait(barrier, group * vec_n - 1)
+    pl.semaphore_wait(barrier, 2 + len(y_sides) + z_sides)
 
     counter = [0]
 
@@ -159,11 +189,6 @@
             device_id_type=MESH,
         )
 
-    z_up = {"gz": lax.rem(me_z + 1, gz_n)}
-    z_down = {"gz": lax.rem(me_z + gz_n - 1, gz_n)}
-    y_up = {"gy": lax.rem(me_y + 1, gy_n)}
-    y_down = {"gy": lax.rem(me_y + gy_n - 1, gy_n)}
-    sibling = {"vec": partners[1]}
     rim_y_copy = remote(links_ref.at[1, :, height - 1], rim_y, y_up)
     rim_z_copy = remote(links_ref.at[2, depth - 1], rim_z, z_up)
     z_copies = [
@@ -178,13 +203,10 @@
     far, relay = [], []
     for k in range(chunks):
         part = pl.ds(k * span, span)
-        far.append(remote(v_ref.at[part], left.at[1, part], {"vec": partners[2]}))
+        far.append(remote(v_ref.at[part], left.at[1, part], across))
         relay.append(remote(left.at[1, part], left.at[2, part], sibling))
     far[0].start()
     rim_y_copy.start()
-    rim_z_copy.start()
-    for copy in z_copies:
-        copy.start()
     for copy in y_copies + far[1:]:
         copy.start()
     near.start()
@@ -333,29 +355,48 @@
         contract(outer, 0, ref, lo, hi, base, True)
         pl.loop(1, chunks)(lambda k: contract(outer, k, ref, lo, hi, base, False))
 
-    pl.loop(0, depth)(pass_x)
+    def turn_round(number):
+        if number:
+            heard(number - 1)
+        greet(number)
+
+    early = min(rounds, depth // 2)
+
+    @pl.loop(0, depth)
+    def _(z):
+        for number in range(early):
+            pl.when(z == 2 * number)(functools.partial(turn_round, number))
+        pass_x(z)
+
+    for number in range(early, rounds):
+        turn_round(number)
     far[0].wait()
     relay[0].start()
     pl.loop(0, depth // 2 - 1)(pass_z)
+    heard(rounds - 1)
+    rim_z_copy.start()
+    for copy in z_copies:
+        copy.start()
+    near.wait()
+    contract_all(0, trans_a, 0, half, 0)
+    rim_y_copy.wait()
+
+    @pl.loop(0, depth // 2)
+    def _(t):
+        put(edge_y, (2 * t + 1,), coefficients(rim_y[2 * t + 1]))
+
+    for copy in y_copies:
+        copy.wait()
+    pl.loop(0, depth // 2)(pass_y)
+    far[1].wait()
+    relay[1].start()
+    rim_z_copy.wait()
     for copy in z_copies:
         copy.wait()
-    rim_z_copy.wait()
     for y in range(1, height, 2):
         put(edge_z, (y,), coefficients(rim_z[y]))
     pass_z_edges()
-    near.wait()
-    contract_all(0, trans_a, 0, half, 0)
-    contract_all(0, trans_b, 0, two, half)
-    rim_y_copy.wait()
-
-    @pl.loop(0, depth // 2)
-    def _(t):
-        put(edge_y, (2 * t + 1,), coefficients(rim_y[2 * t + 1]))
-
-    for copy in y_copies:
-        copy.wait()
-    pl.loop(0, depth // 2)(pass_y)
-    contract_all(0, trans_b, two, half, half)
+    contract_all(0, trans_b, 0, half, half)
 
     left_half = lax.broadcasted_iota(jnp.int32, (1, two), 1) < rows
     kept_near, kept_far = side, pair
@@ -544,19 +585,17 @@
             out_ref[3 * two + part * rows : 3 * two + (part + 1) * rows, columns] = phased
 
     scatter_start(0)
-    for k in range(chunks + 1):
-        if 0 < k < chunks:
+    for k in range(2, chunks + 2):
+        if k < chunks:
             far[k].wait()
             relay[k].start()
-        if k == 2:
-            gather_start(0)
-        if k:
-            relay[k - 1].wait()
-            contract(1, k - 1, trans_a, 0, half, 0, k == 1)
-            contract(1, k - 1, trans_b, 0, half, half, k == 1)
+        relay[k - 2].wait()
+        contract(1, k - 2, trans_a, 0, half, 0, k == 2)
+        contract(1, k - 2, trans_b, 0, half, half, k == 2)
     scatter_start(1)
+    gather_start(0)
+    gather_start(1)
     gather_finish(0)
-    gather_start(1)
     gather_finish(1)
 
 
@@ -616,6 +655,7 @@
             pltpu.SemaphoreType.DMA((remote_count,)),
             pltpu.SemaphoreType.DMA((2, 2, 2, group)),
             pltpu.SemaphoreType.DMA((3, 2, 2, group)),
+            pltpu.SemaphoreType.REGULAR((gy_n // 2 + gz_n,)),
         ],
         compiler_params=pltpu.CompilerParams(
             collective_id=0, has_side_effects=True, vmem_limit_bytes=48 * 1024 * 1024

time: 46.8 us -> 44 us (0.940)
  Pallas kernels: 42.9 us -> 40 us
    pallas_call x1, Pallas kernels: 42.9 us -> 40 us  [body(): pl.pallas_call(functools.partial(kernel, sizes), out_shape=jax.ShapeDtype...]
where the time goes in v2:
time: 44 us; the launch traced here: 43.8 us
  Pallas kernels  40 us (91%)
  local copies, waits for them, and re-layouts  3.74 us (8%)
    pallas_call x1, Pallas kernels, body(): pl.pallas_call(functools.partial(kernel, sizes), out_shape=jax.ShapeDtype...  40 us
    unnamed x7, local copies, waits for them, and re-layouts  3.7 us

profile of v2, /device:TPU:0, one launch (start us, length us, event | category | flops | bytes accessed | tf_op | source)
XLA Modules:
  0.0 43.8 jit_solution(11761722742916242860)
XLA Ops:
  0.0 0.9 %copy.8 = bf16[3,3,3,8,2,128]{5,3,2,1,4,0:T(8,128)(2,1)S(1)} copy(bf16[3,3,3,8,2,128]{5,4,3,2,1,0:T(2,128)(2,1)} %param.5) | data formatting | bytes 221184 | tf_op args[1]
  1.0 1.3 %copy.11 = bf16[64,3,8,2,128]{4,0,1,3,2:T(8,128)(2,1)S(1)} copy(bf16[64,3,8,2,128]{4,3,2,1,0:T(2,128)(2,1)} %param.4) | data formatting | bytes 1572864 | tf_op args[0]
  2.3 0.0 copy-start
  2.3 0.0 copy-start.1
  2.3 0.6 %copy-done = s32[3]{0:T(128)S(1)} copy-done((s32[3]{0:T(128)S(1)}, s32[3]{0:T(128)}, u32[]{:S(2)}) %copy-start) | copy-done | bytes 36
  3.0 0.0 copy-done.1
  3.0 40.0 %shard_map.46 = f32[512,256]{1,0:T(8,128)S(1)} custom-call(s32[3]{0:T(128)S(1)} %copy-done, s32[3]{0:T(128)S(1)} %copy-done.1, bf16[8,2,3,64,128]{4,3,2,1,0:T(8,128)(2,1)S(1)} %bitcast.7, bf16[3,8,2,9,128]{4,3,2,1,0:T(8,128)(2,1)S(1)} %copy.9.links_ref), custom_call_target="tpu_custom_call" | custom-call | tf_op jit(solution)/shard_map/pallas_call | solution.py:622
  43.0 0.8 %copy.13 = f32[4,2,64,256]{3,2,1,0:T(8,128)} copy(f32[4,2,64,256]{3,2,1,0:T(8,128)S(1)} %bitcast.8) | data formatting | bytes 1048576
  (1 shorter events, 0.0 us)
Async XLA Ops:
  2.3 0.7 %copy-start = (s32[3]{0:T(128)S(1)}, s32[3]{0:T(128)}, u32[]{:S(2)}) copy-start(s32[3]{0:T(128)} %momentum_in.1) | copy-start | bytes 40
  2.3 0.7 %copy-start.1 = (s32[3]{0:T(128)S(1)}, s32[3]{0:T(128)}, u32[]{:S(2)}) copy-start(s32[3]{0:T(128)} %directions_in.1) | copy-start | bytes 40

commit v3 on v2

--- a/solution.py
+++ b/solution.py
@@ -39,7 +39,9 @@
     sin_ref,
     trans_a,
     trans_b,
+    trans_c,
     acc,
+    acc_c,
     momentum_ref,
     directions_ref,
     outgo,
@@ -200,11 +202,44 @@
         for z in range(depth)
     ]
     near = remote(v_ref, left.at[0], sibling)
+    stretch = chunks // 2
+
+    def chunk_at(step, owner):
+        return owner * stretch + step if step < stretch else (1 - owner) * stretch + step - stretch
+
+    def pieces(step, owner):
+        first = chunk_at(step, owner) * span
+        if step < stretch:
+            return [(pl.ds(first, span),)]
+        return [(first + dz, y) for dz in range(span) for y in range(1 - dz % 2, height, 2)]
+
+    class Copies:
+        def __init__(self, copies):
+            self.copies = copies
+
+        def start(self):
+            for copy in self.copies:
+                copy.start()
+
+        def wait(self):
+            for copy in self.copies:
+                copy.wait()
+
     far, relay = [], []
-    for k in range(chunks):
-        part = pl.ds(k * span, span)
-        far.append(remote(v_ref.at[part], left.at[1, part], across))
-        relay.append(remote(left.at[1, part], left.at[2, part], sibling))
+    for step in range(chunks):
+        far.append(
+            Copies(
+                [remote(v_ref.at[at], left.at[(1,) + at], across) for at in pieces(step, 1 - pair)]
+            )
+        )
+        relay.append(
+            Copies(
+                [
+                    remote(left.at[(1,) + at], left.at[(2,) + at], sibling)
+                    for at in pieces(step, pair)
+                ]
+            )
+        )
     far[0].start()
     rim_y_copy.start()
     for copy in y_copies + far[1:]:
@@ -265,6 +300,21 @@
                     value, swapped = swap(load(z, y, col, lo))
                     store(trans_a, (z, y, col), 1, lo, value * cosine + swapped * sine)
 
+    def pass_conjugate(t):
+        for dz in range(2):
+            for y in range(dz, height, 2):
+                z = pair * (depth // 2) + 2 * t + dz
+                for lo in range(0, rows, tile):
+                    here = pl.ds(z * height + y, 1)
+                    cosine = cos_ref[here]
+                    sine = sin_ref[here]
+                    for col in range(3):
+                        value, swapped = swap(load(z, y, col, lo))
+                        store(
+                            trans_c, (2 * t + dz, y // 2, col), 0, lo,
+                            value * cosine - swapped * sine,
+                        )
+
     def halo(ref, at):
         return lambda col, lo: ref[at, col, pl.ds(lo, tile)].astype(jnp.float32)
 
@@ -351,6 +401,73 @@
 
     half = 4 * rows
 
+    def contract_far(step):
+        fresh = step == 0
+        first = chunk_at(step, pair) * span
+        columns = slice(two, 2 * two)
+
+        def add(ref, where, parts, sites):
+            a = jnp.concatenate([jnp.concatenate(part, axis=1) for part in parts], axis=0)
+            b = jnp.concatenate(
+                [
+                    jnp.concatenate([left[1 + s, z, y, c] for z, y, c in sites], axis=1)
+                    for s in range(2)
+                ],
+                axis=0,
+            )
+            product = lax.dot_general(
+                a, b, (((1,), (1,)), ((), ())), preferred_element_type=jnp.float32
+            )
+            if fresh:
+                ref[where] = product
+            else:
+                ref[where] += product
+
+        def sites_of(offset):
+            return [
+                (first + dz, y, c)
+                for dz in range(span)
+                for y in range((dz + offset) % 2, height, 2)
+                for c in range(3)
+            ]
+
+        odd, even = sites_of(1), sites_of(0)
+        add(
+            acc,
+            (slice(0, 2 * half), columns),
+            [
+                [trans_a[z, y, c] for z, y, c in odd],
+                [trans_b[z, y // 2, c] for z, y, c in odd],
+            ],
+            odd,
+        )
+        if step < stretch:
+            inner = (step * span) - first
+            product_rows = [
+                [trans_a[z, y, c] for z, y, c in even],
+                [trans_c[z + inner, y // 2, c] for z, y, c in even],
+            ]
+            a = jnp.concatenate(
+                [jnp.concatenate(part, axis=1) for part in product_rows], axis=0
+            )
+            b = jnp.concatenate(
+                [
+                    jnp.concatenate([left[1 + s, z, y, c] for z, y, c in even], axis=1)
+                    for s in range(2)
+                ],
+                axis=0,
+            )
+            product = lax.dot_general(
+                a, b, (((1,), (1,)), ((), ())), preferred_element_type=jnp.float32
+            )
+            acc[0:half, columns] += product[0:half]
+            if fresh:
+                acc_c[0:two] = product[0:two]
+                acc_c[two:] = product[half:]
+            else:
+                acc_c[0:two] += product[0:two]
+                acc_c[two:] += product[half:]
+
     def contract_all(outer, ref, lo, hi, base):
         contract(outer, 0, ref, lo, hi, base, True)
         pl.loop(1, chunks)(lambda k: contract(outer, k, ref, lo, hi, base, False))
@@ -372,6 +489,7 @@
         turn_round(number)
     far[0].wait()
     relay[0].start()
+    pl.loop(0, depth // 4)(pass_conjugate)
     pl.loop(0, depth // 2 - 1)(pass_z)
     heard(rounds - 1)
     rim_z_copy.start()
@@ -417,11 +535,13 @@
         )
 
     def cross(k, phase, step):
-        source = cross_out.at[k - 1, member(step)] if phase == 0 else back_out.at[k - 1]
-        target = cross_in if phase == 0 else back_in
+        if phase == 0:
+            source, target = cross_out[k - 1].at[member(step)], cross_in[k - 1]
+        else:
+            source, target = back_out.at[k - 1], back_in.at[k - 1]
         return pltpu.make_async_remote_copy(
             src_ref=source,
-            dst_ref=target.at[k - 1, me_g],
+            dst_ref=target.at[me_g],
             send_sem=cross_sem.at[k - 1, phase, 0, step],
             recv_sem=cross_sem.at[k - 1, phase, 1, step],
             device_id=place(member(step), k),
@@ -460,7 +580,17 @@
             if_imag = jnp.where(left_half, turn(first), second)
             message = jnp.where(kept == 1, if_real, if_imag).astype(jnp.bfloat16)
             for g in range(group):
-                cross_out[k - 1, g] = message[g * share : (g + 1) * share]
+                cross_out[k - 1][g, 0:share] = message[g * share : (g + 1) * share]
+        if stage == 1:
+            for op in range(2):
+                turned = jnp.transpose(acc_c[op * two : (op + 1) * two])
+                flipped = -turned if op == 0 else turned
+                message = jnp.where(left_half, flipped, -flipped).astype(jnp.bfloat16)
+                for at, k in enumerate(stage_partners[stage]):
+                    for g in range(group):
+                        cross_out[k - 1][g, (op + 1) * share : (op + 2) * share] = message[
+                            at * rows + g * share : at * rows + (g + 1) * share
+                        ]
 
     def scatter_start(stage):
         columns = slice(stage * two, (stage + 1) * two)
@@ -497,9 +627,9 @@
             parts.append(total)
         extra = []
         for k in stage_partners[stage]:
-            total = cross_in[k - 1, 0].astype(jnp.float32)
+            total = cross_in[k - 1][0].astype(jnp.float32)
             for g in range(1, group):
-                total = total + cross_in[k - 1, g].astype(jnp.float32)
+                total = total + cross_in[k - 1][g].astype(jnp.float32)
             extra.append(total)
         if stage == 0:
             adds = [turn(extra[0]), extra[0]]
@@ -513,8 +643,11 @@
             ]
             backs = [jnp.where(left_half, turn(kept_of[0]), kept_of[1])]
         else:
-            parts[4] = parts[4] + jnp.where(left_half, extra[0], turn(extra[1]))
-            parts[5] = parts[5] + jnp.where(left_half, turn(extra[0]), extra[1])
+            for at in range(3):
+                first, second = [total[at * share : (at + 1) * share] for total in extra]
+                low, high = (4, 5) if at == 0 else (2 * at - 2, 2 * at - 1)
+                parts[low] = parts[low] + jnp.where(left_half, first, turn(second))
+                parts[high] = parts[high] + jnp.where(left_half, turn(first), second)
             backs = [
                 jnp.where(left_half, parts[4], turn(parts[5])),
                 jnp.where(left_half, turn(parts[4]), parts[5]),
@@ -590,8 +723,7 @@
             far[k].wait()
             relay[k].start()
         relay[k - 2].wait()
-        contract(1, k - 2, trans_a, 0, half, 0, k == 2)
-        contract(1, k - 2, trans_b, 0, half, half, k == 2)
+        contract_far(k - 2)
     scatter_start(1)
     gather_start(0)
     gather_start(1)
@@ -605,7 +737,7 @@
     gy_n = lax.axis_size("gy")
     vec_n = lax.axis_size("vec")
     group = gz_n * gy_n
-    assert vec_n == 4 and depth % 2 == 0 and height % 2 == 0 and rows % group == 0
+    assert vec_n == 4 and depth % 4 == 0 and height % 2 == 0 and rows % group == 0
     chunks = split_chunks(depth, 4)
     v = jnp.transpose(vectors, (2, 3, 1, 0, 4))
     packed = jnp.transpose(links, (0, 3, 4, 1, 2, 5)).reshape(3, depth, height, 9, lanes)
@@ -613,12 +745,14 @@
     bf16, f32 = jnp.bfloat16, jnp.float32
     share = rows // group
     slots = (8, 6)
-    remote_count = 3 + depth + height + 2 * chunks
+    far_count = chunks // 2 + depth // 2 * (height // 2)
+    remote_count = 3 + depth + height + 2 * far_count
     vmem = pl.BlockSpec(memory_space=pltpu.VMEM)
     hbm = pl.BlockSpec(memory_space=pltpu.HBM)
     sizes = (gz_n, gy_n, vec_n, depth, height, rows, lanes // 2, chunks)
     parts = [pltpu.VMEM((group, n * share, 2 * rows), bf16) for n in slots]
     small = pltpu.VMEM((3, group, share, 2 * rows), bf16)
+    crossing = [pltpu.VMEM((group, n * share, 2 * rows), bf16) for n in (1, 3, 3)]
     out = pl.pallas_call(
         functools.partial(kernel, sizes),
         out_shape=jax.ShapeDtypeStruct((8 * rows, vec_n * rows), f32),
@@ -639,15 +773,17 @@
             pltpu.VMEM((depth * height, lanes), f32),
             pltpu.VMEM((depth, height, 3, 4 * rows, lanes), bf16),
             pltpu.VMEM((depth, height // 2, 3, 4 * rows, lanes), bf16),
+            pltpu.VMEM((depth // 2, height // 2, 3, 2 * rows, lanes), bf16),
             pltpu.VMEM((8 * rows, vec_n * rows), f32),
+            pltpu.VMEM((4 * rows, 2 * rows), f32),
             pltpu.SMEM((3,), jnp.int32),
             pltpu.SMEM((3,), jnp.int32),
             parts,
             parts,
             [pltpu.VMEM((n * share, 2 * rows), bf16) for n in slots],
             parts,
-            small,
-            small,
+            crossing,
+            crossing,
             pltpu.VMEM((3, share, 2 * rows), bf16),
             small,
             pltpu.SemaphoreType.DMA((2,)),

time: 44 us -> 42.2 us (0.959)
  Pallas kernels: 40 us -> 38.2 us
    pallas_call x1, Pallas kernels: 40 us -> 38.2 us  [body(): pl.pallas_call(functools.partial(kernel, sizes), out_shape=jax.ShapeDtype...]
where the time goes in v3:
time: 42.2 us; the launch traced here: 42 us
  Pallas kernels  38.2 us (91%)
  local copies, waits for them, and re-layouts  3.74 us (9%)
    pallas_call x1, Pallas kernels, body(): pl.pallas_call(functools.partial(kernel, sizes), out_shape=jax.ShapeDtype...  38.2 us
    unnamed x7, local copies, waits for them, and re-layouts  3.7 us

profile of v3, /device:TPU:0, one launch (start us, length us, event | category | flops | bytes accessed | tf_op | source)
XLA Modules:
  0.0 42.0 jit_solution(6556563283062366997)
XLA Ops:
  0.0 0.9 %copy.8 = bf16[3,3,3,8,2,128]{5,3,2,1,4,0:T(8,128)(2,1)S(1)} copy(bf16[3,3,3,8,2,128]{5,4,3,2,1,0:T(2,128)(2,1)} %param.5) | data formatting | bytes 221184 | tf_op args[1]
  1.0 1.3 %copy.11 = bf16[64,3,8,2,128]{4,0,1,3,2:T(8,128)(2,1)S(1)} copy(bf16[64,3,8,2,128]{4,3,2,1,0:T(2,128)(2,1)} %param.4) | data formatting | bytes 1572864 | tf_op args[0]
  2.3 0.0 copy-start
  2.3 0.0 copy-start.1
  2.3 0.6 %copy-done = s32[3]{0:T(128)S(1)} copy-done((s32[3]{0:T(128)S(1)}, s32[3]{0:T(128)}, u32[]{:S(2)}) %copy-start) | copy-done | bytes 36
  3.0 0.0 copy-done.1
  3.0 38.2 %shard_map.46 = f32[512,256]{1,0:T(8,128)S(1)} custom-call(s32[3]{0:T(128)S(1)} %copy-done, s32[3]{0:T(128)S(1)} %copy-done.1, bf16[8,2,3,64,128]{4,3,2,1,0:T(8,128)(2,1)S(1)} %bitcast.7, bf16[3,8,2,9,128]{4,3,2,1,0:T(8,128)(2,1)S(1)} %copy.9.links_ref), custom_call_target="tpu_custom_call" | custom-call | tf_op jit(solution)/shard_map/pallas_call | solution.py:756
  41.2 0.8 %copy.13 = f32[4,2,64,256]{3,2,1,0:T(8,128)} copy(f32[4,2,64,256]{3,2,1,0:T(8,128)S(1)} %bitcast.8) | data formatting | bytes 1048576
  (1 shorter events, 0.0 us)
Async XLA Ops:
  2.3 0.7 %copy-start = (s32[3]{0:T(128)S(1)}, s32[3]{0:T(128)}, u32[]{:S(2)}) copy-start(s32[3]{0:T(128)} %momentum_in.1) | copy-start | bytes 40
  2.3 0.7 %copy-start.1 = (s32[3]{0:T(128)S(1)}, s32[3]{0:T(128)}, u32[]{:S(2)}) copy-start(s32[3]{0:T(128)} %directions_in.1) | copy-start | bytes 40
